TPU v7x, 256 devices: a whole 4x4x8 slice. The times are simulated.
256 devices in a mesh: blk: 32 (over x, z), leaf: 4 (over y), samp: 2 (over core).
Axes of the slice: x: 4, y: 4, z: 8, core: 2. Of those that a mesh axis runs over, the one named last changes fastest.
Arguments:
- points: float32 [3, 32768], P(None, ('blk', 'leaf')), may hold values from 0 to 64, as said below
- neighbors: int32 [128, 8], P(('blk', 'leaf')), may hold values from -1 to 127, as said below
- omega: float32 [512, 32768], P(None, ('blk', 'leaf')), may hold values from -6 to 6
- observed: float32 [32768], P(('blk', 'leaf')), may hold values from -6 to 6
- prior_draws: float32 [64, 32768], P('samp', ('blk', 'leaf')), may hold values from -6 to 6
Outputs:
- weights: float32 [64, 32768], P('samp', ('blk', 'leaf'))
- residual: float32 [64, 32768], P('samp', ('blk', 'leaf'))
Inputs may be any that keep to these rules, and one draw needn't show every extreme that they name: Block g's points lie in the unit cell with integer corner (cx, cy, cz), where cx // 2 = g // 4 and 0 <= cy, cz < 3. `neighbors`: row g lists in ascending order every block h whose unit cell touches g's (cells at most one apart in every coordinate, the first taken periodic of period 2 * 32), which includes every block with a point within distance 1 of a point of g, followed by -1 in the unused slots; the relation is symmetric, and every listed block has a slab index h // 4 equal to or cyclically next to g // 4.
All inputs are finite; a program needn't handle non-finite values.
Results may differ from a plain program's by a relative error of at most 0.0003.
Values sent between devices are 32-bit elements; how exact they have to be, the bound alone decides.
A program may use at most 64 MiB of HBM per device.

v0:
```python
import jax
import jax.numpy as jnp
from jax import lax
from jax.sharding import PartitionSpec as P

PB = 256
ITERS = 2
support_radius = 0.8
noise_variance = 1.0
sketch_shift = 1.0
ALL_AXES = ("blk", "leaf", "samp")


def shifted_2(block, axis, distance):
    devices = range(lax.axis_size(axis))
    route = [((i - distance) % len(devices), i) for i in devices]
    return lax.ppermute(block, axis, route)


def wendland(row_points, column_points, period):
    offset = row_points[None, :, :, None] - column_points[:, :, None, :]
    half_period = 0.5 * period
    along_x = jnp.mod(offset[:, 0] + half_period, period) - half_period
    squared = along_x * along_x + offset[:, 1] * offset[:, 1] + offset[:, 2] * offset[:, 2]
    radius = jnp.sqrt(squared) / support_radius
    remain = jnp.maximum(1.0 - radius, 0.0)
    return remain**4 * (4.0 * radius + 1.0)


def high_dot(left, right):
    return jnp.dot(left, right, precision=lax.Precision.HIGHEST, preferred_element_type=jnp.float32)


def shifted(values, offset_by):
    return shifted_2(values, "blk", offset_by)


def beside_all(values):
    slab_values = lax.all_gather(values, "leaf", axis=1, tiled=True)
    return jnp.concatenate([shifted(slab_values, 1), slab_values, shifted(slab_values, -1)], axis=1)


def lower_solve(factor, values):
    return lax.linalg.triangular_solve(factor, values, left_side=True, lower=True)


def local(points, neighbors, omega, observed, prior_draws):
    blk_dev = neighbors.shape[0]
    cycle_count = lax.axis_size("blk")
    slab_blocks = blk_dev * lax.axis_size("leaf")
    period = 2.0 * cycle_count
    own_slab = lax.axis_index("blk")
    n_samp = lax.axis_size("samp")
    samp_idx = lax.axis_index("samp")
    usable = neighbors >= 0
    relative = jnp.mod(neighbors // slab_blocks - own_slab + 1, cycle_count)
    chosen = jnp.where(usable, relative * slab_blocks + jnp.mod(neighbors, slab_blocks), 0)
    usable_weight = usable.astype(jnp.float32)
    reach_points = beside_all(points)
    reach_blocks = reach_points.reshape(3, 3 * slab_blocks, PB).transpose(1, 0, 2)
    row_blocks = points.reshape(3, blk_dev, PB).transpose(1, 0, 2)
    kernel_tile = wendland(row_blocks[0], reach_blocks[chosen[0]], period)
    kernel_tile = kernel_tile * usable_weight[0][:, None, None]

    def apply_kernel(values):
        width = values.shape[0]
        reach = beside_all(values).reshape(width, 3 * slab_blocks, PB)
        picked = jnp.take(reach, chosen[0], axis=1)
        return jnp.einsum("cnj,nij->ci", picked, kernel_tile, precision=lax.Precision.HIGHEST)

    def slot(x):
        zeros = jnp.zeros((n_samp,) + x.shape, x.dtype)
        return lax.dynamic_update_index_in_dim(zeros, x, samp_idx, 0)

    def unslot(xs):
        return lax.dynamic_index_in_dim(xs, samp_idx, 0, keepdims=False)

    def total_per_samp(values):
        return jax.tree.map(unslot, lax.psum(jax.tree.map(slot, values), ALL_AXES))

    sketch = apply_kernel(omega) + sketch_shift * omega
    rhs = observed[None, :] - prior_draws
    half = PB // n_samp
    omega_half = lax.dynamic_slice_in_dim(omega, samp_idx * half, half, axis=1)
    sketch_half = lax.dynamic_slice_in_dim(sketch, samp_idx * half, half, axis=1)
    core_part = high_dot(omega_half, sketch_half.T)
    square_part = high_dot(sketch_half, sketch_half.T)
    rhs_part = slot(high_dot(sketch, rhs.T))
    core_gram, square_gram, rhs_proj = lax.psum((core_part, square_part, rhs_part), ALL_AXES)
    rhs_proj = unslot(rhs_proj)
    core_gram = 0.5 * (core_gram + core_gram.T)
    factor = jnp.linalg.cholesky(core_gram)
    basis = lower_solve(factor, sketch)
    half_solved = lower_solve(factor, square_gram)
    basis_gram = lower_solve(factor, half_solved.T)
    woodbury = noise_variance * jnp.eye(basis.shape[0], dtype=jnp.float32) + 0.5 * (
        basis_gram + basis_gram.T
    )
    wood_factor = jnp.linalg.cholesky(woodbury)

    def precond_from(vectors, projected):
        first_solve = lower_solve(wood_factor, projected)
        solved = lax.linalg.triangular_solve(
            wood_factor, first_solve, left_side=True, lower=True, transpose_a=True
        )
        return (vectors - high_dot(solved.T, basis)) / noise_variance

    residual = rhs
    projected = lower_solve(factor, rhs_proj)
    precond = precond_from(residual, projected)
    direction = precond
    weights = jnp.zeros_like(rhs)
    image = apply_kernel(direction) + noise_variance * direction
    inner_now, curvature, image_proj = total_per_samp(
        (
            jnp.sum(residual * precond, axis=1),
            jnp.sum(direction * image, axis=1),
            high_dot(basis, image.T),
        )
    )
    step_size = inner_now / curvature
    weights = weights + step_size[:, None] * direction
    residual = residual - step_size[:, None] * image
    projected = projected - step_size[None, :] * image_proj
    precond = precond_from(residual, projected)
    inner_next = total_per_samp(jnp.sum(residual * precond, axis=1))
    direction = precond + (inner_next / inner_now)[:, None] * direction
    inner_now = inner_next
    image = apply_kernel(direction) + noise_variance * direction
    curvature = total_per_samp(jnp.sum(direction * image, axis=1))
    step_size = inner_now / curvature
    weights = weights + step_size[:, None] * direction
    residual = residual - step_size[:, None] * image
    return (weights, residual)


def solution(mesh):
    in_specs = (
        P(None, ("blk", "leaf")),
        P(("blk", "leaf"), None),
        P(None, ("blk", "leaf")),
        P(("blk", "leaf")),
        P("samp", ("blk", "leaf")),
    )
    out_specs = (P("samp", ("blk", "leaf")), P("samp", ("blk", "leaf")))
    return jax.shard_map(local, mesh=mesh, in_specs=in_specs, out_specs=out_specs, check_vma=False)
```

profile of v0, /device:TPU:1, one launch (start us, length us, event | category | flops | bytes accessed | tf_op | source)
XLA Modules:
  0.0 1166.5 jit_solution(11193395616657118959)
XLA Ops:
  7.2 2.0 copy.11
  9.3 10.5 all_gather.13
  19.8 7.8 collective-permute-start.3
  27.6 19.4 %all-gather.2.cloned.1.call-done = f32[512,1024]{0,1:T(8,128)} async-done(((f32[512,256]{0,1:T(8,128)}), f32[512,1024]{0,1:T(8,128)}) %all-gather.2.cloned.1.call-update) | async-done | bytes 2097168 | tf_op jit(solution)/shard_map/all_gather | solution.py:39
  47.1 5.2 collective-permute-start.1
  56.0 2.6 multiply_multiply_fusion
  58.7 38.2 %collective-permute-done.1 = f32[512,1024]{0,1:T(8,128)} collective-permute-done((f32[512,1024]{0,1:T(8,128)}, f32[512,1024]{0,1:T(8,128)}, u32[]{:S(2)}, u32[]{:S(2)}) %collective-permute-start.1) | collective-permute-done | bytes 2097184 | tf_op jit(solution)/shard_map/ppermute | solution.py:17
  96.8 5.2 collective-permute-done
  102.0 5.6 pad_maximum_fusion
  107.6 6.5 copy.12
  114.2 5.6 gather_fusion
  119.8 5.5 fusion.17
  125.3 2.0 fusion.65
  127.2 2.0 fusion.63
  130.8 254.7 %all-reduce.8.cloned.1.call-done = (f32[512,512]{1,0:T(8,128)}, f32[2,512,32]{1,2,0:T(8,128)}, f32[512,512]{1,0:T(8,128)}) async-done(((f32[512,512]{1,0:T(8,128)}, f32[2,512,32]{1,2,0:T(8,128)}, f32[512,512]{1,0:T(8,128)}), (f32[512,512]{1,0:T(8,128)}, f32[2,512,32]{1,2,0:T(8,128)}, f32[512,512]{1,0:T(8,128)})) %all-reduce.8.cloned.1.call-update) | async-done | bytes 2228240 | tf_op jit(solution)/shard_map/psum | solution.py:89
  386.4 2.5 copy.14
  389.0 1.8 fusion.28
  390.7 1.4 copy.15
  392.1 1.4 fusion.27
  394.6 11.7 %cholesky.286 = f32[128,128]{1,0:T(8,128)S(1)} custom-call(f32[128,128]{1,0:T(8,128)S(1)} %cholesky.426), custom_call_target="Cholesky" | custom-call | tf_op jit(solution)/shard_map/jit(cholesky)/cholesky | solution.py:92
  406.3 9.8 custom-call.40
  418.8 11.7 %cholesky.305 = f32[128,128]{1,0:T(8,128)S(1)} custom-call(f32[128,128]{1,0:T(8,128)S(1)} %cholesky.430), custom_call_target="Cholesky" | custom-call | tf_op jit(solution)/shard_map/jit(cholesky)/cholesky | solution.py:92
  430.5 10.3 custom-call.41
  443.4 11.7 %cholesky.326 = f32[128,128]{1,0:T(8,128)S(1)} custom-call(f32[128,128]{1,0:T(8,128)S(1)} %cholesky.435), custom_call_target="Cholesky" | custom-call | tf_op jit(solution)/shard_map/jit(cholesky)/cholesky | solution.py:92
  456.4 9.8 custom-call.42
  467.0 1.4 convolution_subtract_fusion.14
  468.4 11.9 %cholesky.343 = f32[128,128]{1,0:T(8,128)S(1)} custom-call(f32[128,128]{1,0:T(8,128)S(1)} %convolution_subtract_fusion.14), custom_call_target="Cholesky" | custom-call | tf_op jit(solution)/shard_map/jit(cholesky)/cholesky | solution.py:92
  485.0 2.4 select_select_fusion.1
  487.4 11.7 %while.15 = (s32[]{:T(128)}, f32[512,512]{1,0:T(8,128)}, s32[4,2]{0,1:T(2,128)S(1)}, f32[4,128,128]{2,1,0:T(8,128)S(1)}, s32[]{:T(128)}) while((s32[]{:T(128)}, f32[512,512]{1,0:T(8,128)}, s32[4,2]{0,1:T(2,128)S(1)}, f32[4,128,128]{2,1,0:T(8,128)S(1)}, s32[]{:T(128)}) %tuple.84), condition=%wide.while_cond.clone, body=%wide.while_body.clone.sunk | while | flops 2 | bytes 131189 | solution.py:44
  488.1 2.3 bitcast_dynamic-update-slice_fusion.4
  491.1 2.3 bitcast_dynamic-update-slice_fusion.4
  494.0 2.3 bitcast_dynamic-update-slice_fusion.4
  496.9 2.2 bitcast_dynamic-update-slice_fusion.4
  499.2 39.3 %custom-call.44 = f32[4,128,128]{1,2,0:T(8,128)S(1)} custom-call(f32[4,128,128]{2,1,0:T(8,128)S(1)} %get-tuple-element.64), custom_call_target="InvertDiagBlocksLowerTriangular" | custom-call | tf_op jit(solution)/shard_map/triangular_solve/custom-call.3 | solution.py:44
  553.4 1.5 convolution_subtract_fusion.4
  557.4 1.6 fusion.26
  560.4 1.4 fusion.24
  562.8 12.1 %cholesky.358 = f32[128,128]{1,0:T(8,128)S(1)} custom-call(f32[128,128]{1,0:T(8,128)S(1)} %cholesky.439), custom_call_target="Cholesky" | custom-call | tf_op jit(solution)/shard_map/jit(cholesky)/cholesky | solution.py:99
  575.6 9.8 custom-call.45
  588.8 11.7 %cholesky.377 = f32[128,128]{1,0:T(8,128)S(1)} custom-call(f32[128,128]{1,0:T(8,128)S(1)} %cholesky.443), custom_call_target="Cholesky" | custom-call | tf_op jit(solution)/shard_map/jit(cholesky)/cholesky | solution.py:99
  601.2 9.8 custom-call.46
  613.5 11.9 %cholesky.398 = f32[128,128]{1,0:T(8,128)S(1)} custom-call(f32[128,128]{1,0:T(8,128)S(1)} %cholesky.448), custom_call_target="Cholesky" | custom-call | tf_op jit(solution)/shard_map/jit(cholesky)/cholesky | solution.py:99
  626.1 9.8 custom-call.47
  637.3 11.7 %cholesky.415 = f32[128,128]{1,0:T(8,128)S(1)} custom-call(f32[128,128]{1,0:T(8,128)S(1)} %convolution_subtract_fusion.13), custom_call_target="Cholesky" | custom-call | tf_op jit(solution)/shard_map/jit(cholesky)/cholesky | solution.py:99
  652.4 1.4 select_select_fusion
  653.8 10.8 while.16
  665.4 40.3 %custom-call.50 = f32[4,128,128]{1,2,0:T(8,128)S(1)} custom-call(f32[4,128,128]{2,1,0:T(8,128)} %copy-done.26), custom_call_target="InvertDiagBlocksLowerTriangular" | custom-call | tf_op jit(solution)/shard_map/triangular_solve/custom-call.9 | solution.py:103
  710.9 1.4 convolution_subtract_fusion.16
  712.3 9.4 all_gather.14
  721.7 5.5 collective-permute-start.5
  727.8 1.4 collective-permute-done.5
  729.1 5.2 collective-permute-done.4
  735.1 2.4 gather_fusion.2
  737.5 3.6 multiply_reduce_fusion.3
  746.6 75.2 %all-reduce.1 = (f32[2,32]{1,0:T(2,128)}, f32[2,32]{1,0:T(2,128)}) all-reduce(f32[2,32]{1,0:T(2,128)} %dynamic_update_slice.22, f32[2,32]{1,0:T(2,128)} %dynamic_update_slice.21), channel_id=1, replica_groups=mesh['blk'=32,'leaf'=4,'samp'=2] {'blk','leaf','samp'}, use_global_device_ids=true, to_apply=%region_14.20 | all-reduce | flops 128 | bytes 1024 | tf_op jit(solution)/shard_map/psum | solution.py:79
  823.0 1.5 multiply_subtract_fusion.1
  824.5 156.1 %all-reduce.6.cloned.1.call-done = f32[2,512,32]{1,2,0:T(8,128)} async-done(((f32[2,512,32]{1,2,0:T(8,128)}), f32[2,512,32]{1,2,0:T(8,128)}) %all-reduce.6.cloned.1.call-update) | async-done | bytes 131088 | tf_op jit(solution)/shard_map/psum | solution.py:79
  985.2 75.9 %psum.62 = f32[2,32]{1,0:T(2,128)S(1)} all-reduce(f32[2,32]{1,0:T(2,128)S(1)} %dynamic_update_slice.24), channel_id=1, replica_groups=mesh['blk'=32,'leaf'=4,'samp'=2] {'blk','leaf','samp'}, use_global_device_ids=true, to_apply=%region_17.23 | all-reduce | flops 64 | bytes 512 | tf_op jit(solution)/shard_map/psum | solution.py:79
  1062.0 9.1 all_gather.15
  1071.1 1.6 collective-permute-start.7
  1072.9 2.4 collective-permute-done.7
  1075.2 4.6 collective-permute-done.6
  1080.5 2.0 multiply_reduce_fusion
  1082.6 76.1 %psum.63 = f32[2,32]{1,0:T(2,128)S(1)} all-reduce(f32[2,32]{1,0:T(2,128)S(1)} %dynamic_update_slice.25), channel_id=1, replica_groups=mesh['blk'=32,'leaf'=4,'samp'=2] {'blk','leaf','samp'}, use_global_device_ids=true, to_apply=%region_19.25 | all-reduce | flops 64 | bytes 512 | tf_op jit(solution)/shard_map/psum | solution.py:79
  (244 shorter events, 80.5 us)
Async XLA Ops:
  7.2 39.9 %all-gather.2.cloned.1.call-start = ((), (), s32[]{:S(2)}) async-start(), calls=%async_computation | async-start | bytes 2621440 | tf_op jit(solution)/shard_map/all_gather | solution.py:39
  9.3 376.3 %all-reduce.8.cloned.1.call-start = ((), (), s32[]{:S(2)}) async-start(), calls=%async_computation.2 | async-start | bytes 4456448 | tf_op jit(solution)/shard_map/psum | solution.py:89
  19.8 34.3 %collective-permute-start.3 = (f32[3,1024]{1,0:T(4,128)S(1)}, f32[3,1024]{1,0:T(4,128)S(1)}, u32[]{:S(2)}, u32[]{:S(2)}) collective-permute-start(f32[3,1024]{1,0:T(4,128)S(1)} %all_gather.13), channel_id=1, source_target_pairs={{8,0},{16,8},{24,16},{32,24},{40,32},{48,40},{56,48},{64,56},{72,6... | collective-permute-start | bytes 36872 | tf_op jit(solution)/shard_map/ppermute | solution.py:17
  27.6 26.5 %collective-permute-start.2 = (f32[3,1024]{1,0:T(4,128)S(1)}, f32[3,1024]{1,0:T(4,128)S(1)}, u32[]{:S(2)}, u32[]{:S(2)}) collective-permute-start(f32[3,1024]{1,0:T(4,128)S(1)} %all_gather.13), channel_id=1, source_target_pairs={{248,0},{0,8},{8,16},{16,24},{24,32},{32,40},{40,48},{48,56},{56,6... | collective-permute-start | bytes 36872 | tf_op jit(solution)/shard_map/ppermute | solution.py:17
  47.1 49.8 %collective-permute-start.1 = (f32[512,1024]{0,1:T(8,128)}, f32[512,1024]{0,1:T(8,128)}, u32[]{:S(2)}, u32[]{:S(2)}) collective-permute-start(f32[512,1024]{0,1:T(8,128)} %all-gather.2.cloned.1.call-done), channel_id=1, source_target_pairs={{8,0},{16,8},{24,16},{32,24},{40,32},{48,40},{56,48},{64,56},{72,6... | collective-permute-start | bytes 6291464 | tf_op jit(solution)/shard_map/ppermute | solution.py:17
  52.2 49.8 %collective-permute-start = (f32[512,1024]{0,1:T(8,128)}, f32[512,1024]{0,1:T(8,128)}, u32[]{:S(2)}, u32[]{:S(2)}) collective-permute-start(f32[512,1024]{0,1:T(8,128)} %all-gather.2.cloned.1.call-done), channel_id=1, source_target_pairs={{248,0},{0,8},{8,16},{16,24},{24,32},{32,40},{40,48},{48,56},{56,6... | collective-permute-start | bytes 6291464 | tf_op jit(solution)/shard_map/ppermute | solution.py:17
  54.1 65.7 %copy-start.36 = (pred[8]{0:T(512)(128)(4,1)}, pred[8]{0:T(512)(128)(4,1)S(1)}, u32[]{:S(2)}) copy-start(pred[8]{0:T(512)(128)(4,1)S(1)} %compare_and_fusion) | copy-start | bytes 28
  56.0 46.0 %copy-start.11 = (f32[512,1024]{0,1:T(8,128)S(1)}, f32[512,1024]{0,1:T(8,128)}, u32[]{:S(2)}) copy-start(f32[512,1024]{0,1:T(8,128)} %all-gather.2.cloned.1.call-done) | copy-start | bytes 6291460
  114.2 5.6 copy-start.7
  125.2 4.0 copy-start
  125.2 4.0 copy-start.24
  125.2 4.0 copy-start.33
  129.9 0.7 copy-start.19
  130.5 850.0 %all-reduce.6.cloned.1.call-start = ((), (), s32[]{:S(2)}) async-start(), calls=%async_computation.1 | async-start | bytes 262144 | tf_op jit(solution)/shard_map/psum | solution.py:79
  393.5 1.0 copy-start.9
  441.1 1.0 copy-start.3
  443.3 95.2 %copy-start.1 = (f32[512,256]{1,0:T(8,128)S(1)}, f32[512,256]{1,0:T(8,128)}, u32[]{:S(2)}) copy-start(f32[512,256]{1,0:T(8,128)} %copy-done) | copy-start | bytes 1572868
  499.1 48.0 %copy-start.32 = (s32[4,2]{0,1:T(2,128)}, s32[4,2]{0,1:T(2,128)S(1)}, u32[]{:S(2)}) copy-start(s32[4,2]{0,1:T(2,128)S(1)} %get-tuple-element.250) | copy-start | bytes 100
  538.5 6.7 copy-start.2
  538.5 8.7 copy-start.15
  540.4 2.6 copy-start.23
  541.7 1.3 copy-start.25
  545.2 3.2 copy-start.12
  545.8 1.4 copy-start.20
  551.9 3.4 copy-start.5
  553.4 1.9 copy-start.6
  555.3 0.7 copy-start.10
  561.8 1.0 copy-start.8
  588.1 0.7 copy-start.16
  649.1 3.3 copy-start.4
  664.7 0.7 copy-start.26
  705.7 21.5 %copy-start.38 = (s32[8]{0:T(128)S(1)}, s32[8]{0:T(128)}, u32[]{:S(2)}) copy-start(s32[8]{0:T(128)} %get-tuple-element.93) | copy-start | bytes 100
  712.3 16.8 %copy-start.17 = (f32[32,256]{1,0:T(8,128)}, f32[32,256]{1,0:T(8,128)S(1)}, u32[]{:S(2)}) copy-start(f32[32,256]{1,0:T(8,128)S(1)} %convolution_subtract_fusion.16) | copy-start | bytes 98308
  721.7 7.5 collective-permute-start.5
  727.2 7.1 collective-permute-start.4
  737.5 4.3 copy-start.13
  737.5 4.3 copy-start.21
  737.5 4.3 copy-start.28
  741.1 0.7 copy-start.27
  822.4 0.5 copy-start.34
  980.6 4.1 copy-start.14
  980.6 4.1 copy-start.22
  980.6 4.1 copy-start.29
  980.6 4.1 copy-start.30
  981.6 79.5 %copy-start.39 = (f32[2,32]{1,0:T(2,128)S(1)}, f32[2,32]{1,0:T(2,128)}, u32[]{:S(2)}) copy-start(f32[2,32]{1,0:T(2,128)} %get-tuple-element.89) | copy-start | bytes 772
  983.5 97.0 %copy-start.37 = (pred[8]{0:T(512)(128)(4,1)S(1)}, pred[8]{0:T(512)(128)(4,1)}, u32[]{:S(2)}) copy-start(pred[8]{0:T(512)(128)(4,1)} %copy-done.36) | copy-start | bytes 28
  1071.1 87.7 %copy-start.18 = (f32[32,256]{1,0:T(8,128)S(1)}, f32[32,256]{1,0:T(8,128)}, u32[]{:S(2)}) copy-start(f32[32,256]{1,0:T(8,128)} %copy-done.17) | copy-start | bytes 98308
  1071.1 87.7 %copy-start.31 = (f32[32,256]{1,0:T(8,128)S(1)}, f32[32,256]{1,0:T(8,128)}, u32[]{:S(2)}) copy-start(f32[32,256]{1,0:T(8,128)} %multiply_subtract_fusion.1) | copy-start | bytes 98308
  1071.1 87.7 %copy-start.35 = (f32[32]{0:T(128)S(1)}, f32[32]{0:T(128)}, u32[]{:S(2)}) copy-start(f32[32]{0:T(128)} %copy-done.34) | copy-start | bytes 388
  1071.1 4.1 collective-permute-start.7
  1072.6 7.1 collective-permute-start.6
Sparse Core Ops, SparseCore 0:
  9.8 37.2 all-gather.1
  130.7 254.8 all-reduce.7
  743.1 237.3 all-reduce.5
where the time goes:
time: 1180 us; the launch traced here: 1170 us
  waiting for transfers between devices  487 us (41%)
  other arithmetic  267 us (23%)
  blocking collectives  256 us (22%)
  local copies, waits for them, and re-layouts  59.4 us (5%)
  matrix products  55.7 us (5%)
  starting transfers between devices  20.6 us (2%)
  between operations  20.6 us (2%)
    psum x1, waiting for transfers between devices, local(): lax.psum((core_part, square_part, rhs_part), ALL_AXES)  255 us
    psum x3, blocking collectives, total_per_samp(): return jax.tree.map(unslot, lax.psum(jax.tree.map(slot, values), ALL_AXES))  227 us
    psum x1, waiting for transfers between devices, total_per_samp(): return jax.tree.map(unslot, lax.psum(jax.tree.map(slot, values), ALL_AXES))  156 us
    another operation x14, other arithmetic, local(): factor = jnp.linalg.cholesky(core_gram)  80.3 us
    another operation x15, other arithmetic, local(): wood_factor = jnp.linalg.cholesky(woodbury)  79.8 us
    ppermute x8, waiting for transfers between devices, shifted_2(): return lax.ppermute(block, axis, route)  56.8 us
    another operation x4, other arithmetic, lower_solve(): lax.linalg.triangular_solve(factor, values, left_side=True, lower=True)  41.8 us
    another operation x2, other arithmetic, precond_from(): lax.linalg.triangular_solve(wood_factor, first_solve, left_side=True, low...  41.7 us
  transfers between devices with their start and end apart: 11, of which 9 were waited for; matrix products, arithmetic and copies ran while one was open for 1% of the time, Pallas kernels for 0%

commit v1 on v0

--- a/solution.py
+++ b/solution.py
@@ -9,6 +9,11 @@
 noise_variance = 1.0
 sketch_shift = 1.0
 ALL_AXES = ("blk", "leaf", "samp")
+
+
+def one_after_other(array, axis_one, axis_two):
+    partial = lax.psum(array, axis_one)
+    return lax.psum(partial, axis_two)
 
 
 def shifted_2(block, axis, distance):
@@ -86,7 +91,9 @@
     core_part = high_dot(omega_half, sketch_half.T)
     square_part = high_dot(sketch_half, sketch_half.T)
     rhs_part = slot(high_dot(sketch, rhs.T))
-    core_gram, square_gram, rhs_proj = lax.psum((core_part, square_part, rhs_part), ALL_AXES)
+    core_gram, square_gram, rhs_proj = one_after_other(
+        (core_part, square_part, rhs_part), ("leaf", "samp"), "blk"
+    )
     rhs_proj = unslot(rhs_proj)
     core_gram = 0.5 * (core_gram + core_gram.T)
     factor = jnp.linalg.cholesky(core_gram)

time: 1180 us -> 1150 us (0.975)
  waiting for transfers between devices: 487 us -> 451 us
    psum x1 -> x2, waiting for transfers between devices: 255 us -> 220 us  [the longest x1 156 us: one_after_other(): return lax.psum(partial, axis_two)]
  transfers between devices with their start and end apart: 11 -> 12, of which waited for: 9 -> 10; matrix products, arithmetic and copies ran while one was open for 1% -> 1% of each run, Pallas kernels for 0% -> 0%
where the time goes in v1:
time: 1150 us; the launch traced here: 1140 us
  waiting for transfers between devices  451 us (39%)
  other arithmetic  267 us (23%)
  blocking collectives  263 us (23%)
  local copies, waits for them, and re-layouts  60 us (5%)
  matrix products  55.7 us (5%)
  between operations  20.5 us (2%)
  starting transfers between devices  18.1 us (2%)
    psum x3, blocking collectives, total_per_samp(): return jax.tree.map(unslot, lax.psum(jax.tree.map(slot, values), ALL_AXES))  234 us
    psum x1, waiting for transfers between devices, one_after_other(): return lax.psum(partial, axis_two)  156 us
    psum x1, waiting for transfers between devices, total_per_samp(): return jax.tree.map(unslot, lax.psum(jax.tree.map(slot, values), ALL_AXES))  155 us
    another operation x14, other arithmetic, local(): factor = jnp.linalg.cholesky(core_gram)  80.4 us
    another operation x15, other arithmetic, local(): wood_factor = jnp.linalg.cholesky(woodbury)  79.8 us
    psum x1, waiting for transfers between devices, one_after_other(): partial = lax.psum(array, axis_one)  63.9 us
    ppermute x8, waiting for transfers between devices, shifted_2(): return lax.ppermute(block, axis, route)  56.8 us
    another operation x4, other arithmetic, lower_solve(): lax.linalg.triangular_solve(factor, values, left_side=True, lower=True)  41.8 us
  transfers between devices with their start and end apart: 12, of which 10 were waited for; matrix products, arithmetic and copies ran while one was open for 1% of the time, Pallas kernels for 0%

profile of v1, /device:TPU:1, one launch (start us, length us, event | category | flops | bytes accessed | tf_op | source)
XLA Modules:
  0.0 1135.4 jit_solution(16777836520307094748)
XLA Ops:
  7.2 2.0 copy.11
  9.3 10.5 all_gather.13
  19.9 7.8 collective-permute-start.3
  27.6 19.4 %all-gather.2.cloned.1.call-done = f32[512,1024]{0,1:T(8,128)} async-done(((f32[512,256]{0,1:T(8,128)}), f32[512,1024]{0,1:T(8,128)}) %all-gather.2.cloned.1.call-update) | async-done | bytes 2097168 | tf_op jit(solution)/shard_map/all_gather | solution.py:44
  47.1 5.2 collective-permute-start.1
  56.0 2.6 multiply_multiply_fusion
  58.7 38.2 %collective-permute-done.1 = f32[512,1024]{0,1:T(8,128)} collective-permute-done((f32[512,1024]{0,1:T(8,128)}, f32[512,1024]{0,1:T(8,128)}, u32[]{:S(2)}, u32[]{:S(2)}) %collective-permute-start.1) | collective-permute-done | bytes 2097184 | tf_op jit(solution)/shard_map/ppermute | solution.py:22
  96.8 5.2 collective-permute-done
  102.0 5.6 pad_maximum_fusion
  107.6 6.5 copy.12
  114.2 5.6 gather_fusion
  119.8 5.5 fusion.17
  125.3 2.0 fusion.65
  127.3 2.0 fusion.63
  130.6 63.9 %all-reduce.12.cloned.1.call-done = (f32[512,512]{1,0:T(8,128)}, f32[2,512,32]{1,2,0:T(8,128)}, f32[512,512]{1,0:T(8,128)}) async-done(((f32[512,512]{1,0:T(8,128)}, f32[2,512,32]{1,2,0:T(8,128)}, f32[512,512]{1,0:T(8,128)}), (f32[512,512]{1,0:T(8,128)}, f32[2,512,32]{1,2,0:T(8,128)}, f32[512,512]{1,0:T(8,128)})) %all-reduce.12.cloned.1.call-update) | async-done | bytes 2228240 | tf_op jit(solution)/shard_map/psum | solution.py:15
  194.8 156.1 %all-reduce.10.cloned.1.call-done = (f32[512,512]{1,0:T(8,128)}, f32[2,512,32]{1,2,0:T(8,128)}, f32[512,512]{1,0:T(8,128)}) async-done(((f32[512,512]{1,0:T(8,128)}, f32[2,512,32]{1,2,0:T(8,128)}, f32[512,512]{1,0:T(8,128)}), (f32[512,512]{1,0:T(8,128)}, f32[2,512,32]{1,2,0:T(8,128)}, f32[512,512]{1,0:T(8,128)})) %all-reduce.10.cloned.1.call-update) | async-done | bytes 2228240 | tf_op jit(solution)/shard_map/psum | solution.py:16
  351.7 2.6 copy.14
  354.3 1.8 fusion.28
  356.1 1.4 copy.15
  357.5 1.4 fusion.27
  360.0 11.7 %cholesky.286 = f32[128,128]{1,0:T(8,128)S(1)} custom-call(f32[128,128]{1,0:T(8,128)S(1)} %cholesky.426), custom_call_target="Cholesky" | custom-call | tf_op jit(solution)/shard_map/jit(cholesky)/cholesky | solution.py:99
  371.7 9.8 custom-call.40
  384.2 11.7 %cholesky.305 = f32[128,128]{1,0:T(8,128)S(1)} custom-call(f32[128,128]{1,0:T(8,128)S(1)} %cholesky.430), custom_call_target="Cholesky" | custom-call | tf_op jit(solution)/shard_map/jit(cholesky)/cholesky | solution.py:99
  395.9 10.3 custom-call.41
  408.7 11.7 %cholesky.326 = f32[128,128]{1,0:T(8,128)S(1)} custom-call(f32[128,128]{1,0:T(8,128)S(1)} %cholesky.435), custom_call_target="Cholesky" | custom-call | tf_op jit(solution)/shard_map/jit(cholesky)/cholesky | solution.py:99
  421.8 9.8 custom-call.42
  432.5 1.4 convolution_subtract_fusion.14
  433.9 11.9 %cholesky.343 = f32[128,128]{1,0:T(8,128)S(1)} custom-call(f32[128,128]{1,0:T(8,128)S(1)} %convolution_subtract_fusion.14), custom_call_target="Cholesky" | custom-call | tf_op jit(solution)/shard_map/jit(cholesky)/cholesky | solution.py:99
  450.4 2.4 select_select_fusion.1
  452.8 12.2 %while.15 = (s32[]{:T(128)}, f32[512,512]{1,0:T(8,128)}, s32[4,2]{0,1:T(2,128)S(1)}, f32[4,128,128]{2,1,0:T(8,128)S(1)}, s32[]{:T(128)}) while((s32[]{:T(128)}, f32[512,512]{1,0:T(8,128)}, s32[4,2]{0,1:T(2,128)S(1)}, f32[4,128,128]{2,1,0:T(8,128)S(1)}, s32[]{:T(128)}) %tuple.84), condition=%wide.while_cond.clone, body=%wide.while_body.clone.sunk | while | flops 2 | bytes 131189 | solution.py:49
  453.5 2.4 bitcast_dynamic-update-slice_fusion.4
  456.6 2.4 bitcast_dynamic-update-slice_fusion.4
  459.6 2.4 bitcast_dynamic-update-slice_fusion.4
  462.7 2.3 bitcast_dynamic-update-slice_fusion.4
  465.0 39.3 %custom-call.44 = f32[4,128,128]{1,2,0:T(8,128)S(1)} custom-call(f32[4,128,128]{2,1,0:T(8,128)S(1)} %get-tuple-element.64), custom_call_target="InvertDiagBlocksLowerTriangular" | custom-call | tf_op jit(solution)/shard_map/triangular_solve/custom-call.3 | solution.py:49
  519.2 1.5 convolution_subtract_fusion.4
  523.2 1.6 fusion.26
  526.2 1.4 fusion.24
  528.6 12.1 %cholesky.358 = f32[128,128]{1,0:T(8,128)S(1)} custom-call(f32[128,128]{1,0:T(8,128)S(1)} %cholesky.439), custom_call_target="Cholesky" | custom-call | tf_op jit(solution)/shard_map/jit(cholesky)/cholesky | solution.py:106
  541.4 9.8 custom-call.45
  554.6 11.7 %cholesky.377 = f32[128,128]{1,0:T(8,128)S(1)} custom-call(f32[128,128]{1,0:T(8,128)S(1)} %cholesky.443), custom_call_target="Cholesky" | custom-call | tf_op jit(solution)/shard_map/jit(cholesky)/cholesky | solution.py:106
  567.0 9.8 custom-call.46
  579.3 11.9 %cholesky.398 = f32[128,128]{1,0:T(8,128)S(1)} custom-call(f32[128,128]{1,0:T(8,128)S(1)} %cholesky.448), custom_call_target="Cholesky" | custom-call | tf_op jit(solution)/shard_map/jit(cholesky)/cholesky | solution.py:106
  591.9 9.8 custom-call.47
  603.2 11.7 %cholesky.415 = f32[128,128]{1,0:T(8,128)S(1)} custom-call(f32[128,128]{1,0:T(8,128)S(1)} %convolution_subtract_fusion.13), custom_call_target="Cholesky" | custom-call | tf_op jit(solution)/shard_map/jit(cholesky)/cholesky | solution.py:106
  618.2 1.4 select_select_fusion
  619.6 10.8 while.16
  631.0 40.3 %custom-call.50 = f32[4,128,128]{1,2,0:T(8,128)S(1)} custom-call(f32[4,128,128]{2,1,0:T(8,128)} %copy-done.26), custom_call_target="InvertDiagBlocksLowerTriangular" | custom-call | tf_op jit(solution)/shard_map/triangular_solve/custom-call.9 | solution.py:110
  676.6 1.4 convolution_subtract_fusion.16
  678.0 9.4 all_gather.14
  687.4 3.0 collective-permute-start.5
  692.4 5.2 collective-permute-done.4
  698.4 2.4 gather_fusion.2
  700.7 3.6 multiply_reduce_fusion.3
  710.0 82.1 %all-reduce.1 = (f32[2,32]{1,0:T(2,128)}, f32[2,32]{1,0:T(2,128)}) all-reduce(f32[2,32]{1,0:T(2,128)} %dynamic_update_slice.22, f32[2,32]{1,0:T(2,128)} %dynamic_update_slice.21), channel_id=1, replica_groups=mesh['blk'=32,'leaf'=4,'samp'=2] {'blk','leaf','samp'}, use_global_device_ids=true, to_apply=%region_17.23 | all-reduce | flops 128 | bytes 1024 | tf_op jit(solution)/shard_map/psum | solution.py:84
  793.3 1.5 multiply_subtract_fusion.1
  794.8 154.8 %all-reduce.8.cloned.1.call-done = f32[2,512,32]{1,2,0:T(8,128)} async-done(((f32[2,512,32]{1,2,0:T(8,128)}), f32[2,512,32]{1,2,0:T(8,128)}) %all-reduce.8.cloned.1.call-update) | async-done | bytes 131088 | tf_op jit(solution)/shard_map/psum | solution.py:84
  954.2 75.9 %psum.86 = f32[2,32]{1,0:T(2,128)S(1)} all-reduce(f32[2,32]{1,0:T(2,128)S(1)} %dynamic_update_slice.24), channel_id=1, replica_groups=mesh['blk'=32,'leaf'=4,'samp'=2] {'blk','leaf','samp'}, use_global_device_ids=true, to_apply=%region_20.26 | all-reduce | flops 64 | bytes 512 | tf_op jit(solution)/shard_map/psum | solution.py:84
  1030.9 9.1 all_gather.15
  1040.0 1.6 collective-permute-start.7
  1041.8 2.4 collective-permute-done.7
  1044.2 4.6 collective-permute-done.6
  1049.5 2.0 multiply_reduce_fusion
  1051.6 76.1 %psum.87 = f32[2,32]{1,0:T(2,128)S(1)} all-reduce(f32[2,32]{1,0:T(2,128)S(1)} %dynamic_update_slice.25), channel_id=1, replica_groups=mesh['blk'=32,'leaf'=4,'samp'=2] {'blk','leaf','samp'}, use_global_device_ids=true, to_apply=%region_22.28 | all-reduce | flops 64 | bytes 512 | tf_op jit(solution)/shard_map/psum | solution.py:84
  (247 shorter events, 82.0 us)
Async XLA Ops:
  7.2 39.9 %all-gather.2.cloned.1.call-start = ((), (), s32[]{:S(2)}) async-start(), calls=%async_computation | async-start | bytes 2621440 | tf_op jit(solution)/shard_map/all_gather | solution.py:44
  9.3 185.2 %all-reduce.12.cloned.1.call-start = ((), (), s32[]{:S(2)}) async-start(), calls=%async_computation.3 | async-start | bytes 4456448 | tf_op jit(solution)/shard_map/psum | solution.py:15
  19.9 34.3 %collective-permute-start.3 = (f32[3,1024]{1,0:T(4,128)S(1)}, f32[3,1024]{1,0:T(4,128)S(1)}, u32[]{:S(2)}, u32[]{:S(2)}) collective-permute-start(f32[3,1024]{1,0:T(4,128)S(1)} %all_gather.13), channel_id=1, source_target_pairs={{8,0},{16,8},{24,16},{32,24},{40,32},{48,40},{56,48},{64,56},{72,6... | collective-permute-start | bytes 36872 | tf_op jit(solution)/shard_map/ppermute | solution.py:22
  27.6 26.5 %collective-permute-start.2 = (f32[3,1024]{1,0:T(4,128)S(1)}, f32[3,1024]{1,0:T(4,128)S(1)}, u32[]{:S(2)}, u32[]{:S(2)}) collective-permute-start(f32[3,1024]{1,0:T(4,128)S(1)} %all_gather.13), channel_id=1, source_target_pairs={{248,0},{0,8},{8,16},{16,24},{24,32},{32,40},{40,48},{48,56},{56,6... | collective-permute-start | bytes 36872 | tf_op jit(solution)/shard_map/ppermute | solution.py:22
  47.1 49.8 %collective-permute-start.1 = (f32[512,1024]{0,1:T(8,128)}, f32[512,1024]{0,1:T(8,128)}, u32[]{:S(2)}, u32[]{:S(2)}) collective-permute-start(f32[512,1024]{0,1:T(8,128)} %all-gather.2.cloned.1.call-done), channel_id=1, source_target_pairs={{8,0},{16,8},{24,16},{32,24},{40,32},{48,40},{56,48},{64,56},{72,6... | collective-permute-start | bytes 6291464 | tf_op jit(solution)/shard_map/ppermute | solution.py:22
  52.2 49.8 %collective-permute-start = (f32[512,1024]{0,1:T(8,128)}, f32[512,1024]{0,1:T(8,128)}, u32[]{:S(2)}, u32[]{:S(2)}) collective-permute-start(f32[512,1024]{0,1:T(8,128)} %all-gather.2.cloned.1.call-done), channel_id=1, source_target_pairs={{248,0},{0,8},{8,16},{16,24},{24,32},{32,40},{40,48},{48,56},{56,6... | collective-permute-start | bytes 6291464 | tf_op jit(solution)/shard_map/ppermute | solution.py:22
  54.1 65.7 %copy-start.36 = (pred[8]{0:T(512)(128)(4,1)}, pred[8]{0:T(512)(128)(4,1)S(1)}, u32[]{:S(2)}) copy-start(pred[8]{0:T(512)(128)(4,1)S(1)} %compare_and_fusion) | copy-start | bytes 28
  56.0 46.0 %copy-start.11 = (f32[512,1024]{0,1:T(8,128)S(1)}, f32[512,1024]{0,1:T(8,128)}, u32[]{:S(2)}) copy-start(f32[512,1024]{0,1:T(8,128)} %all-gather.2.cloned.1.call-done) | copy-start | bytes 6291460
  114.2 5.6 copy-start.7
  125.2 4.0 copy-start
  125.3 4.0 copy-start.24
  125.3 4.0 copy-start.33
  129.9 0.7 copy-start.19
  130.6 220.3 %all-reduce.10.cloned.1.call-start = ((), (), s32[]{:S(2)}) async-start(), calls=%async_computation.2 | async-start | bytes 4456448 | tf_op jit(solution)/shard_map/psum | solution.py:16
  194.5 755.1 %all-reduce.8.cloned.1.call-start = ((), (), s32[]{:S(2)}) async-start(), calls=%async_computation.1 | async-start | bytes 262144 | tf_op jit(solution)/shard_map/psum | solution.py:84
  358.9 1.0 copy-start.9
  406.4 1.0 copy-start.3
  408.7 95.6 %copy-start.1 = (f32[512,256]{1,0:T(8,128)S(1)}, f32[512,256]{1,0:T(8,128)}, u32[]{:S(2)}) copy-start(f32[512,256]{1,0:T(8,128)} %copy-done) | copy-start | bytes 1572868
  465.0 48.0 %copy-start.32 = (s32[4,2]{0,1:T(2,128)}, s32[4,2]{0,1:T(2,128)S(1)}, u32[]{:S(2)}) copy-start(s32[4,2]{0,1:T(2,128)S(1)} %get-tuple-element.267) | copy-start | bytes 100
  504.4 6.7 copy-start.2
  504.4 8.7 copy-start.15
  506.2 2.6 copy-start.23
  507.6 1.3 copy-start.25
  511.1 3.2 copy-start.12
  511.7 1.4 copy-start.20
  517.8 3.4 copy-start.5
  519.2 1.9 copy-start.6
  521.2 0.7 copy-start.10
  527.6 1.0 copy-start.8
  553.9 0.7 copy-start.16
  614.9 3.3 copy-start.4
  630.3 0.7 copy-start.26
  671.4 19.0 %copy-start.38 = (s32[8]{0:T(128)S(1)}, s32[8]{0:T(128)}, u32[]{:S(2)}) copy-start(s32[8]{0:T(128)} %get-tuple-element.96) | copy-start | bytes 100
  678.0 14.4 %copy-start.17 = (f32[32,256]{1,0:T(8,128)}, f32[32,256]{1,0:T(8,128)S(1)}, u32[]{:S(2)}) copy-start(f32[32,256]{1,0:T(8,128)S(1)} %convolution_subtract_fusion.16) | copy-start | bytes 98308
  687.4 4.9 collective-permute-start.5
  690.4 7.1 collective-permute-start.4
  700.7 4.3 copy-start.13
  700.7 4.3 copy-start.21
  700.7 4.3 copy-start.28
  704.4 0.7 copy-start.27
  792.8 0.5 copy-start.34
  949.6 4.1 copy-start.14
  949.6 4.1 copy-start.22
  949.6 4.1 copy-start.29
  949.6 4.1 copy-start.30
  950.6 79.5 %copy-start.39 = (f32[2,32]{1,0:T(2,128)S(1)}, f32[2,32]{1,0:T(2,128)}, u32[]{:S(2)}) copy-start(f32[2,32]{1,0:T(2,128)} %get-tuple-element.89) | copy-start | bytes 772
  952.5 97.0 %copy-start.37 = (pred[8]{0:T(512)(128)(4,1)S(1)}, pred[8]{0:T(512)(128)(4,1)}, u32[]{:S(2)}) copy-start(pred[8]{0:T(512)(128)(4,1)} %copy-done.36) | copy-start | bytes 28
  1040.0 87.7 %copy-start.18 = (f32[32,256]{1,0:T(8,128)S(1)}, f32[32,256]{1,0:T(8,128)}, u32[]{:S(2)}) copy-start(f32[32,256]{1,0:T(8,128)} %copy-done.17) | copy-start | bytes 98308
  1040.0 87.7 %copy-start.31 = (f32[32,256]{1,0:T(8,128)S(1)}, f32[32,256]{1,0:T(8,128)}, u32[]{:S(2)}) copy-start(f32[32,256]{1,0:T(8,128)} %multiply_subtract_fusion.1) | copy-start | bytes 98308
  1040.0 87.7 %copy-start.35 = (f32[32]{0:T(128)S(1)}, f32[32]{0:T(128)}, u32[]{:S(2)}) copy-start(f32[32]{0:T(128)} %copy-done.34) | copy-start | bytes 388
  1040.0 4.1 collective-permute-start.7
  1041.6 7.1 collective-permute-start.6
Sparse Core Ops, SparseCore 0:
  9.8 37.2 all-gather.1
  130.7 63.7 all-reduce.11
  198.8 152.0 all-reduce.9
  706.4 243.0 all-reduce.7
